TPU v7x, 32 devices: a whole 2x2x4 slice. The times are simulated.
32 devices in a mesh: lon: 8 (over z, y), lat: 4 (over x, core).
Axes of the slice: x: 2, y: 2, z: 4, core: 2. Of those that a mesh axis runs over, the one named last changes fastest.
Arguments:
- sample_deviations: float32 [32, 32, 32, 1024], P(None, None, 'lat', 'lon'), may hold values from -6 to 6
- east_courant: float32 [32, 32, 1024], P(None, 'lat', 'lon'), may hold values from -0.45 to 0.45
- north_courant: float32 [32, 32, 1024], P(None, 'lat', 'lon'), may hold values from -0.45 to 0.45
- production: float32 [32, 32, 1024], P(None, 'lat', 'lon'), may hold values from -1.8 to 1.8
- loss_rate: float32 [32, 32, 1024], P(None, 'lat', 'lon'), may hold values from 0.02 to 0.3
- entry_count: int32 [32], P(('lon', 'lat')), may hold values from 24 to 48, as said below
- entry_row: int32 [1536], P(('lon', 'lat')), may hold values from 0 to 7
- entry_block: int32 [1536], P(('lon', 'lat')), may hold values from 0 to 15
- path_weight: bfloat16 [1536, 128, 128], P(('lon', 'lat')), may hold values from 0 to 0.15234375
- observed: float32 [16384], P(('lon', 'lat')), may hold values from -288 to 288
- obs_var: float32 [16384], P(('lon', 'lat')), may hold values from 64 to 4608, as said below
Outputs:
- updated_samples: float32 [32, 32, 32, 1024], P(None, None, 'lat', 'lon')
- prior_samples_in_path_space: float32 [32, 16384], P(None, ('lon', 'lat'))
- scaled_innovation: float32 [16384], P(('lon', 'lat'))
Inputs may be any that keep to these rules, and one draw needn't show every extreme that they name: `entry_count`: live crossing slots of each tile; some tile has all 48 live in every draw. `obs_var`: positive.
All inputs are finite; a program needn't handle non-finite values.
Results may differ from a plain program's by a relative error of at most 0.0025.
Values sent between devices are 32-bit elements; how exact they have to be, the bound alone decides.
No kernel may reach another device: no remote copies, remote signals or barrier semaphores. Data moves between devices by JAX's collectives and lax.ppermute only.
A program may use at most 64 MiB of HBM per device.

v0:
```python
import math
import jax
import jax.numpy as jnp
from jax import lax
from jax.sharding import PartitionSpec as P

ALTITUDE_LAYERS = 32
RAY_BLOCK = 128
BLOCKS_DEV = 4
SLOTS_TILE = 48
highest = lax.Precision.HIGHEST


def extended(x, sides, width, wrap):
    for axis, dim in sides:
        size, length = (lax.axis_size(axis), x.shape[dim])
        up = [(i, (i + 1) % size) for i in range(size if wrap else size - 1)]
        down = [(j, i) for i, j in up]
        last = lax.slice_in_dim(x, length - width, length, axis=dim)
        initial = lax.slice_in_dim(x, 0, width, axis=dim)
        before = lax.ppermute(last, axis, up)
        after = lax.ppermute(initial, axis, down)
        x = jnp.concatenate([before, x, after], axis=dim)
    return x


def advance(
    plasma_concentration,
    west_cell,
    east_cell,
    south_cell,
    north_cell,
    east_speed,
    north_speed,
    source,
    loss_rate,
):
    advected = (
        plasma_concentration
        - jnp.maximum(east_speed, 0.0) * (plasma_concentration - west_cell)
        - jnp.minimum(east_speed, 0.0) * (east_cell - plasma_concentration)
    )
    advected = (
        advected
        - jnp.maximum(north_speed, 0.0) * (plasma_concentration - south_cell)
        - jnp.minimum(north_speed, 0.0) * (north_cell - plasma_concentration)
    )
    return (1.0 - loss_rate) * advected + source


def analysis_weights(gram_sum, pull_sum):
    member_total = gram_sum.shape[0]
    identity = jnp.eye(member_total, dtype=gram_sum.dtype)
    factor_low = jnp.linalg.cholesky(gram_sum + (member_total - 1.0) * identity)
    halfway = lax.linalg.triangular_solve(factor_low, pull_sum[:, None], left_side=True, lower=True)
    mean_weights = lax.linalg.triangular_solve(
        factor_low, halfway, left_side=True, lower=True, transpose_a=True
    )
    inverse = lax.linalg.triangular_solve(factor_low, identity, left_side=True, lower=True)
    return mean_weights + math.sqrt(member_total - 1.0) * inverse.T


def ray_moments(ensemble, observed, obs_var):
    ray_mean = jnp.mean(ensemble, axis=0)
    spread = ensemble - ray_mean
    misfit = observed - ray_mean
    gram_sum = jnp.dot(spread / obs_var, spread.T, precision=highest)
    pull_sum = jnp.dot(spread, misfit / obs_var, precision=highest)
    return (gram_sum, pull_sum, misfit / jnp.sqrt(obs_var))


def per_device(
    sample_deviations,
    east_courant,
    north_courant,
    production,
    loss_rate,
    entry_count,
    entry_row,
    entry_block,
    path_weight,
    observed,
    obs_var,
):
    ensemble_size = sample_deviations.shape[0]
    plasma_concentration = sample_deviations
    for repeat in range(2):
        lon_framed = extended(plasma_concentration, (("lon", 3),), 1, True)
        lat_framed = extended(plasma_concentration, (("lat", 2),), 1, False)
        plasma_concentration = advance(
            plasma_concentration,
            lon_framed[..., :-2],
            lon_framed[..., 2:],
            lat_framed[..., :-2, :],
            lat_framed[..., 2:, :],
            east_courant,
            north_courant,
            production,
            loss_rate,
        )
    column_integral_total = (
        jnp.sum(plasma_concentration, axis=1) / math.sqrt(ALTITUDE_LAYERS)
    ).astype(jnp.bfloat16)
    picked = jnp.take(column_integral_total, entry_row, axis=1)
    partial_value = jnp.einsum(
        "mkc,kcr->kmr", picked, path_weight, preferred_element_type=jnp.float32
    )
    lat_size = lax.axis_size("lat")
    col_blocks = BLOCKS_DEV * lat_size
    live_slots = (jnp.arange(SLOTS_TILE) < entry_count[0]).astype(jnp.float32)
    slot_select = (entry_block[None, :] == jnp.arange(col_blocks)[:, None]).astype(
        jnp.float32
    ) * live_slots[None, :]
    summed = jnp.einsum("bk,kmr->mbr", slot_select, partial_value, precision=highest).reshape(
        ensemble_size, col_blocks * RAY_BLOCK
    )
    prior_samples_in_path_space = lax.psum_scatter(summed, "lat", scatter_dimension=1, tiled=True)
    gram_sum, pull_sum, scaled_innovation = ray_moments(
        prior_samples_in_path_space, observed, obs_var
    )
    gram_sum, pull_sum = lax.psum((gram_sum, pull_sum), ("lon", "lat"))
    transform = analysis_weights(gram_sum, pull_sum)
    raveled_grid_vector = plasma_concentration.reshape(ensemble_size, -1)
    centre = jnp.mean(raveled_grid_vector, axis=0)
    anomalies = raveled_grid_vector - centre
    updated_samples = centre + jnp.dot(transform.T, anomalies, precision=highest)
    return (
        updated_samples.reshape(plasma_concentration.shape),
        prior_samples_in_path_space,
        scaled_innovation,
    )


def solution(mesh):
    in_specs = (
        P(None, None, "lat", "lon"),
        P(None, "lat", "lon"),
        P(None, "lat", "lon"),
        P(None, "lat", "lon"),
        P(None, "lat", "lon"),
        P(("lon", "lat")),
        P(("lon", "lat")),
        P(("lon", "lat")),
        P(("lon", "lat"), None, None),
        P(("lon", "lat")),
        P(("lon", "lat")),
    )
    out_specs = (P(None, None, "lat", "lon"), P(None, ("lon", "lat")), P(("lon", "lat")))
    return jax.shard_map(
        per_device, mesh=mesh, in_specs=in_specs, out_specs=out_specs, check_vma=False
    )
```

profile of v0, /device:TPU:0, one launch (start us, length us, event | category | flops | bytes accessed | tf_op | source)
XLA Modules:
  0.0 201.4 jit_solution(16212824213112395093)
XLA Ops:
  7.2 8.1 %fusion.64 = (f32[32,32,8,1]{3,2,1,0:T(8,128)}, f32[32,32,8,1]{3,2,1,0:T(8,128)}) fusion(f32[32,32,8,128]{3,2,1,0:T(8,128)} %param.11), kind=kLoop, calls=%fused_computation.101 | loop fusion | bytes 131072 | tf_op jit(solution)/shard_map/slice | solution.py:19
  15.3 3.2 %copy.180 = f32[32,32,8,1]{1,2,3,0:T(8,128)S(1)} copy(f32[32,32,8,1]{3,2,1,0:T(8,128)} %get-tuple-element.12) | data formatting | bytes 65536
  18.6 3.0 %collective-permute-start = (f32[32,32,8,1]{1,2,3,0:T(8,128)S(1)}, f32[32,32,8,1]{1,2,3,0:T(8,128)}, u32[]{:S(2)}, u32[]{:S(2)}) collective-permute-start(f32[32,32,8,1]{1,2,3,0:T(8,128)S(1)} %copy.180), channel_id=1, source_target_pairs={{0,4},{4,8},{8,12},{12,16},{16,20},{20,24},{24,28},{28,0},{1,5},{5... | collective-permute-start | bytes 98312 | tf_op jit(solution)/shard_map/ppermute | solution.py:21
  21.6 3.8 %copy.181 = f32[32,32,8,1]{1,2,3,0:T(8,128)} copy(f32[32,32,8,1]{3,2,1,0:T(8,128)} %get-tuple-element.13) | data formatting | bytes 65536
  25.5 3.1 %collective-permute-start.1 = (f32[32,32,8,1]{1,2,3,0:T(8,128)}, f32[32,32,8,1]{1,2,3,0:T(8,128)}, u32[]{:S(2)}, u32[]{:S(2)}) collective-permute-start(f32[32,32,8,1]{1,2,3,0:T(8,128)} %copy.181), channel_id=1, source_target_pairs={{4,0},{8,4},{12,8},{16,12},{20,16},{24,20},{28,24},{0,28},{5,1},{9... | collective-permute-start | bytes 98312 | tf_op jit(solution)/shard_map/ppermute | solution.py:22
  28.6 5.4 %fusion.65 = (f32[32,32,1,128]{3,2,1,0:T(1,128)}, f32[32,32,1,128]{3,2,1,0:T(1,128)}) fusion(f32[32,32,8,128]{3,2,1,0:T(8,128)} %param.11), kind=kLoop, calls=%fused_computation.102 | loop fusion | bytes 2097152 | tf_op jit(solution)/shard_map/slice | solution.py:19
  34.0 1.5 collective-permute-start.2
  35.5 1.3 collective-permute-start.3
  36.9 0.9 broadcast_maximum_fusion
  38.5 3.8 %copy.159 = f32[32,32,8,1]{3,2,1,0:T(8,128)} copy(f32[32,32,8,1]{1,2,3,0:T(8,128)} %collective-permute-done) | data formatting | bytes 65536 | tf_op jit(solution)/shard_map/ppermute | solution.py:21
  42.3 3.8 %copy.161 = f32[32,32,8,1]{3,2,1,0:T(8,128)} copy(f32[32,32,8,1]{1,2,3,0:T(8,128)} %collective-permute-done.1) | data formatting | bytes 65536 | tf_op jit(solution)/shard_map/ppermute | solution.py:22
  46.2 12.7 %fusion.19 = f32[32,32,8,128]{3,2,1,0:T(8,128)S(1)} fusion(f32[32,32,8,128]{3,2,1,0:T(8,128)} %param.11, f32[32,32,1,128]{3,2,1,0:T(1,128)S(1)} %bitcast.69, f32[32,32,1,128]{3,2,1,0:T(1,128)S(1)} %bitcast.68, f32[32,32,8,1]{3,2,1,0:T(8,128)} %copy.161, f32[32,32,8,1]{3,2,1,0:T(8,128)} %copy.159, f32[32,8,128]{2,1,0:T(8,128)S(1)} %copy-done.2, ...), kind=kLoop, calls=%fused_computation.27 | loop fusion | flops 18874368 | bytes 10289152 | tf_op jit(solution)/shard_map/add | solution.py:48
  58.8 2.4 %fusion.63 = (f32[32,32,1,128]{3,2,1,0:T(1,128)}, f32[32,32,1,128]{3,2,1,0:T(1,128)}) fusion(f32[32,32,8,128]{3,2,1,0:T(8,128)S(1)} %fusion.19), kind=kLoop, calls=%fused_computation.100 | loop fusion | bytes 2097152 | tf_op jit(solution)/shard_map/slice | solution.py:19
  61.2 4.7 %collective-permute-start.6 = (f32[32,32,1,128]{3,1,2,0:T(8,128)}, f32[32,32,1,128]{3,1,2,0:T(8,128)S(1)}, u32[]{:S(2)}, u32[]{:S(2)}) collective-permute-start(f32[32,32,1,128]{3,1,2,0:T(8,128)} %bitcast.2), channel_id=1, source_target_pairs={{0,1},{1,2},{2,3},{4,5},{5,6},{6,7},{8,9},{9,10},{10,11},{12,13},{... | collective-permute-start | bytes 1572872 | tf_op jit(solution)/shard_map/ppermute | solution.py:21
  65.9 1.3 collective-permute-start.7
  67.2 4.9 %fusion.62 = (f32[32,32,8,1]{3,2,1,0:T(8,128)}, f32[32,32,8,1]{3,2,1,0:T(8,128)}) fusion(f32[32,32,8,128]{3,2,1,0:T(8,128)S(1)} %fusion.19), kind=kLoop, calls=%fused_computation.99 | loop fusion | bytes 131072 | tf_op jit(solution)/shard_map/slice | solution.py:19
  72.1 3.2 %copy.166 = f32[32,32,8,1]{1,2,3,0:T(8,128)S(1)} copy(f32[32,32,8,1]{3,2,1,0:T(8,128)} %get-tuple-element.8) | data formatting | bytes 65536 | tf_op jit(solution)/shard_map/slice | solution.py:19
  75.4 3.8 %copy.168 = f32[32,32,8,1]{1,2,3,0:T(8,128)} copy(f32[32,32,8,1]{3,2,1,0:T(8,128)} %get-tuple-element.9) | data formatting | bytes 65536 | tf_op jit(solution)/shard_map/slice | solution.py:20
  79.2 4.7 %collective-permute-start.5 = (f32[32,32,8,1]{1,2,3,0:T(8,128)}, f32[32,32,8,1]{1,2,3,0:T(8,128)}, u32[]{:S(2)}, u32[]{:S(2)}) collective-permute-start(f32[32,32,8,1]{1,2,3,0:T(8,128)} %copy.168), channel_id=1, source_target_pairs={{4,0},{8,4},{12,8},{16,12},{20,16},{24,20},{28,24},{0,28},{5,1},{9... | collective-permute-start | bytes 98312 | tf_op jit(solution)/shard_map/ppermute | solution.py:22
  83.9 3.8 %copy.167 = f32[32,32,8,1]{3,2,1,0:T(8,128)} copy(f32[32,32,8,1]{1,2,3,0:T(8,128)} %collective-permute-done.4) | data formatting | bytes 65536 | tf_op jit(solution)/shard_map/ppermute | solution.py:21
  87.7 3.9 %copy.169 = f32[32,32,8,1]{3,2,1,0:T(8,128)} copy(f32[32,32,8,1]{1,2,3,0:T(8,128)} %collective-permute-done.5) | data formatting | bytes 65536 | tf_op jit(solution)/shard_map/ppermute | solution.py:22
  91.6 15.0 %fusion.60 = (f32[32,8,128]{2,1,0:T(8,128)S(1)}, f32[32,8,128]{2,1,0:T(8,128)S(1)}, f32[32,32,8,128]{3,2,1,0:T(8,128)}) fusion(f32[32,8,128]{2,1,0:T(8,128)S(1)} %copy-done.2, f32[32,32,8,128]{3,2,1,0:T(8,128)} %copy-done.1, f32[32,32,1,128]{3,2,1,0:T(1,128)S(1)} %bitcast.67, f32[32,8,128]{2,1,0:T(8,128)S(1)} %get-tuple-element.19, ...), kind=kLoop, calls=%fused_computation.98 | loop fusion | flops 20905984 | bytes 10551296 | tf_op jit(solution)/shard_map/reduce_sum | solution.py:124
  107.9 1.0 fusion.32
  109.7 23.5 %reduce-scatter.2.cloned.1.call-done = f32[32,512]{1,0:T(8,128)} async-done(((f32[32,2048]{1,0:T(8,128)}), f32[32,512]{1,0:T(8,128)}) %reduce-scatter.2.cloned.1.call-update) | async-done | bytes 65552 | tf_op jit(solution)/shard_map/reduce_scatter | solution.py:117
  133.2 0.9 reduce_sum.29
  134.7 1.1 fusion.40
  135.8 1.0 convolution_bitcast_fusion
  136.8 39.5 %all-reduce = (f32[32,32]{1,0:T(8,128)S(1)}, f32[32]{0:T(128)S(1)}) all-reduce(f32[32,32]{1,0:T(8,128)S(1)} %fusion.40, f32[32]{0:T(128)S(1)} %convolution_bitcast_fusion), channel_id=1, replica_groups=mesh['lon'=8,'lat'=4] {'lon','lat'}, use_global_device_ids=true, to_apply=%region_4.5 | all-reduce | flops 1056 | bytes 8448 | tf_op jit(solution)/shard_map/psum | solution.py:121
  176.3 2.9 %cholesky.17 = f32[32,32]{1,0:T(8,128)S(1)} custom-call(f32[32,32]{1,0:T(8,128)S(1)} %fusion.51), custom_call_target="Cholesky" | custom-call | tf_op jit(solution)/shard_map/jit(cholesky)/cholesky | solution.py:54
  180.6 2.4 %custom-call.10 = f32[1,32,32]{1,2,0:T(8,128)S(1)} custom-call(f32[1,32,32]{2,1,0:T(8,128)S(1)} %fusion.47), custom_call_target="InvertDiagBlocksLowerTriangular" | custom-call | tf_op jit(solution)/shard_map/triangular_solve | solution.py:56
  183.6 8.3 %fusion.29 = f32[4,8,256,128]{3,1,2,0:T(8,128)S(1)} fusion(f32[32,32]{1,0:T(8,128)S(1)} %fusion.31, f32[4,8,256,128]{3,2,1,0:T(8,128)} %bitcast.62, f32[32768]{0:T(1024)S(1)} %multiply_bitcast_fusion), kind=kOutput, calls=%fused_computation.40 | convolution fusion | flops 404750336 | bytes 8523776 | tf_op jit(solution)/shard_map/dot_general | solution.py:126
  191.8 2.8 %copy.186 = f32[4,8,256,128]{3,2,1,0:T(8,128)} copy(f32[4,8,256,128]{3,1,2,0:T(8,128)S(1)} %fusion.29) | data formatting | bytes 8388608
  (49 shorter events, 4.8 us)
Async XLA Ops:
  7.2 100.1 %copy-start = (bf16[48,128,128]{2,1,0:T(8,128)(2,1)S(1)}, bf16[48,128,128]{2,1,0:T(8,128)(2,1)}, u32[]{:S(2)}) copy-start(bf16[48,128,128]{2,1,0:T(8,128)(2,1)} %param.19) | copy-start | bytes 4718596
  7.2 126.0 %reduce-scatter.2.cloned.1.call-start = ((), (), s32[]{:S(2)}) async-start(), calls=%async_computation.1 | async-start | bytes 327680 | tf_op jit(solution)/shard_map/reduce_scatter | solution.py:117
  18.6 18.2 %copy-start.3 = (f32[32,8,128]{2,1,0:T(8,128)S(1)}, f32[32,8,128]{2,1,0:T(8,128)}, u32[]{:S(2)}) copy-start(f32[32,8,128]{2,1,0:T(8,128)} %param.15) | copy-start | bytes 393220
  18.6 18.2 %copy-start.8 = (s32[48]{0:T(128)S(1)}, s32[48]{0:T(128)}, u32[]{:S(2)}) copy-start(s32[48]{0:T(128)} %param.17) | copy-start | bytes 580
  18.6 18.3 %copy-start.4 = (f32[32,8,128]{2,1,0:T(8,128)S(1)}, f32[32,8,128]{2,1,0:T(8,128)}, u32[]{:S(2)}) copy-start(f32[32,8,128]{2,1,0:T(8,128)} %param.13) | copy-start | bytes 393220
  18.6 19.9 %collective-permute-start = (f32[32,32,8,1]{1,2,3,0:T(8,128)S(1)}, f32[32,32,8,1]{1,2,3,0:T(8,128)}, u32[]{:S(2)}, u32[]{:S(2)}) collective-permute-start(f32[32,32,8,1]{1,2,3,0:T(8,128)S(1)} %copy.180), channel_id=1, source_target_pairs={{0,4},{4,8},{8,12},{12,16},{16,20},{20,24},{24,28},{28,0},{1,5},{5... | collective-permute-start | bytes 98312 | tf_op jit(solution)/shard_map/ppermute | solution.py:21
  25.5 16.8 %collective-permute-start.1 = (f32[32,32,8,1]{1,2,3,0:T(8,128)}, f32[32,32,8,1]{1,2,3,0:T(8,128)}, u32[]{:S(2)}, u32[]{:S(2)}) collective-permute-start(f32[32,32,8,1]{1,2,3,0:T(8,128)} %copy.181), channel_id=1, source_target_pairs={{4,0},{8,4},{12,8},{16,12},{20,16},{24,20},{28,24},{0,28},{5,1},{9... | collective-permute-start | bytes 98312 | tf_op jit(solution)/shard_map/ppermute | solution.py:22
  34.0 12.1 %collective-permute-start.2 = (f32[32,32,1,128]{3,1,2,0:T(8,128)}, f32[32,32,1,128]{3,1,2,0:T(8,128)S(1)}, u32[]{:S(2)}, u32[]{:S(2)}) collective-permute-start(f32[32,32,1,128]{3,1,2,0:T(8,128)} %bitcast.20), channel_id=1, source_target_pairs={{0,1},{1,2},{2,3},{4,5},{5,6},{6,7},{8,9},{9,10},{10,11},{12,13},{... | collective-permute-start | bytes 1572872 | tf_op jit(solution)/shard_map/ppermute | solution.py:21
  35.5 10.7 %collective-permute-start.3 = (f32[32,32,1,128]{3,1,2,0:T(8,128)}, f32[32,32,1,128]{3,1,2,0:T(8,128)S(1)}, u32[]{:S(2)}, u32[]{:S(2)}) collective-permute-start(f32[32,32,1,128]{3,1,2,0:T(8,128)} %bitcast.21), channel_id=1, source_target_pairs={{1,0},{2,1},{3,2},{5,4},{6,5},{7,6},{9,8},{10,9},{11,10},{13,12},{... | collective-permute-start | bytes 1572872 | tf_op jit(solution)/shard_map/ppermute | solution.py:22
  38.5 7.7 %copy-start.2 = (f32[32,8,128]{2,1,0:T(8,128)S(1)}, f32[32,8,128]{2,1,0:T(8,128)}, u32[]{:S(2)}) copy-start(f32[32,8,128]{2,1,0:T(8,128)} %param.14) | copy-start | bytes 393220
  58.8 13.3 %copy-start.1 = (f32[32,32,8,128]{3,2,1,0:T(8,128)}, f32[32,32,8,128]{3,2,1,0:T(8,128)S(1)}, u32[]{:S(2)}) copy-start(f32[32,32,8,128]{3,2,1,0:T(8,128)S(1)} %fusion.19) | copy-start | bytes 12582916
  61.2 30.4 %collective-permute-start.6 = (f32[32,32,1,128]{3,1,2,0:T(8,128)}, f32[32,32,1,128]{3,1,2,0:T(8,128)S(1)}, u32[]{:S(2)}, u32[]{:S(2)}) collective-permute-start(f32[32,32,1,128]{3,1,2,0:T(8,128)} %bitcast.2), channel_id=1, source_target_pairs={{0,1},{1,2},{2,3},{4,5},{5,6},{6,7},{8,9},{9,10},{10,11},{12,13},{... | collective-permute-start | bytes 1572872 | tf_op jit(solution)/shard_map/ppermute | solution.py:21
  65.9 25.7 %collective-permute-start.7 = (f32[32,32,1,128]{3,1,2,0:T(8,128)}, f32[32,32,1,128]{3,1,2,0:T(8,128)S(1)}, u32[]{:S(2)}, u32[]{:S(2)}) collective-permute-start(f32[32,32,1,128]{3,1,2,0:T(8,128)} %bitcast.4), channel_id=1, source_target_pairs={{1,0},{2,1},{3,2},{5,4},{6,5},{7,6},{9,8},{10,9},{11,10},{13,12},{... | collective-permute-start | bytes 1572872 | tf_op jit(solution)/shard_map/ppermute | solution.py:22
  75.3 8.6 %collective-permute-start.4 = (f32[32,32,8,1]{1,2,3,0:T(8,128)S(1)}, f32[32,32,8,1]{1,2,3,0:T(8,128)}, u32[]{:S(2)}, u32[]{:S(2)}) collective-permute-start(f32[32,32,8,1]{1,2,3,0:T(8,128)S(1)} %copy.166), channel_id=1, source_target_pairs={{0,4},{4,8},{8,12},{12,16},{16,20},{20,24},{24,28},{28,0},{1,5},{5... | collective-permute-start | bytes 98312 | tf_op jit(solution)/shard_map/ppermute | solution.py:21
  79.2 8.5 %collective-permute-start.5 = (f32[32,32,8,1]{1,2,3,0:T(8,128)}, f32[32,32,8,1]{1,2,3,0:T(8,128)}, u32[]{:S(2)}, u32[]{:S(2)}) collective-permute-start(f32[32,32,8,1]{1,2,3,0:T(8,128)} %copy.168), channel_id=1, source_target_pairs={{4,0},{8,4},{12,8},{16,12},{20,16},{24,20},{28,24},{0,28},{5,1},{9... | collective-permute-start | bytes 98312 | tf_op jit(solution)/shard_map/ppermute | solution.py:22
  91.6 16.3 %copy-start.7 = (s32[48]{0:T(128)S(1)}, s32[48]{0:T(128)}, u32[]{:S(2)}) copy-start(s32[48]{0:T(128)} %param.18) | copy-start | bytes 580
  106.6 27.5 %copy-start.5 = (f32[512]{0:T(512)S(1)}, f32[512]{0:T(512)}, u32[]{:S(2)}) copy-start(f32[512]{0:T(512)} %param.20) | copy-start | bytes 6148
  106.6 27.5 %copy-start.6 = (f32[512]{0:T(512)S(1)}, f32[512]{0:T(512)}, u32[]{:S(2)}) copy-start(f32[512]{0:T(512)} %param.21) | copy-start | bytes 6148
Sparse Core Ops, SparseCore 0:
  109.8 23.3 reduce-scatter.1
where the time goes:
time: 202 us; the launch traced here: 201 us
  local copies, waits for them, and re-layouts  54.5 us (27%)
  blocking collectives  39.5 us (20%)
  other arithmetic  36.8 us (18%)
  waiting for transfers between devices  23.6 us (12%)
  starting transfers between devices  19.7 us (10%)
  between operations  14.9 us (7%)
  matrix products  12.5 us (6%)
    psum x1, blocking collectives, per_device(): gram_sum, pull_sum = lax.psum((gram_sum, pull_sum), ('lon', 'lat'))  39.5 us
    slice x5, local copies, waits for them, and re-layouts, extended(): last = lax.slice_in_dim(x, length - width, length, axis=dim)  24 us
    reduce_scatter x1, waiting for transfers between devices, per_device(): lax.psum_scatter(summed, 'lat', scatter_dimension=1, tiled=True)  23.5 us
    reduce_sum x1, other arithmetic, per_device(): centre = jnp.mean(raveled_grid_vector, axis=0)  15 us
    add x1, other arithmetic, advance(): return (1.0 - loss_rate) * advected + source  12.7 us
    unnamed x22, local copies, waits for them, and re-layouts  10.7 us
    ppermute x4, starting transfers between devices, extended(): after = lax.ppermute(initial, axis, down)  10.4 us
    ppermute x4, starting transfers between devices, extended(): before = lax.ppermute(last, axis, up)  9.26 us
  transfers between devices with their start and end apart: 9, of which 1 were waited for; matrix products, arithmetic and copies ran while one was open for 19% of the time, Pallas kernels for 0%

commit v1 on v0

--- a/solution.py
+++ b/solution.py
@@ -118,7 +118,7 @@
     gram_sum, pull_sum, scaled_innovation = ray_moments(
         prior_samples_in_path_space, observed, obs_var
     )
-    gram_sum, pull_sum = lax.psum((gram_sum, pull_sum), ("lon", "lat"))
+    gram_sum, pull_sum = lax.psum(lax.psum((gram_sum, pull_sum), axis_name="lat"), axis_name="lon")
     transform = analysis_weights(gram_sum, pull_sum)
     raveled_grid_vector = plasma_concentration.reshape(ensemble_size, -1)
     centre = jnp.mean(raveled_grid_vector, axis=0)

time: 202 us -> 210 us (1.040)
  blocking collectives: 39.5 us -> 47.4 us
    psum x1 -> x2, blocking collectives: 39.5 us -> 47.4 us  [the longest x1 37.2 us: per_device(): lax.psum(lax.psum((gram_sum, pull_sum), axis_name='lat'), axis_name='lon')]
  transfers between devices with their start and end apart: 9 -> 9, of which waited for: 1 -> 1; matrix products, arithmetic and copies ran while one was open for 19% -> 18% of each run, Pallas kernels for 0% -> 0%
where the time goes in v1:
time: 210 us; the launch traced here: 209 us
  local copies, waits for them, and re-layouts  54.5 us (26%)
  blocking collectives  47.4 us (23%)
  other arithmetic  36.8 us (18%)
  waiting for transfers between devices  23.6 us (11%)
  starting transfers between devices  19.7 us (9%)
  between operations  14.9 us (7%)
  matrix products  12.5 us (6%)
    psum x1, blocking collectives, per_device(): lax.psum(lax.psum((gram_sum, pull_sum), axis_name='lat'), axis_name='lon')  37.2 us
    slice x5, local copies, waits for them, and re-layouts, extended(): last = lax.slice_in_dim(x, length - width, length, axis=dim)  24 us
    reduce_scatter x1, waiting for transfers between devices, per_device(): lax.psum_scatter(summed, 'lat', scatter_dimension=1, tiled=True)  23.5 us
    reduce_sum x1, other arithmetic, per_device(): centre = jnp.mean(raveled_grid_vector, axis=0)  15 us
    add x1, other arithmetic, advance(): return (1.0 - loss_rate) * advected + source  12.7 us
    unnamed x22, local copies, waits for them, and re-layouts  10.7 us
    ppermute x4, starting transfers between devices, extended(): after = lax.ppermute(initial, axis, down)  10.4 us
    psum x1, blocking collectives, per_device(): lax.psum((gram_sum, pull_sum), axis_name='lat')  10.3 us
  transfers between devices with their start and end apart: 9, of which 1 were waited for; matrix products, arithmetic and copies ran while one was open for 18% of the time, Pallas kernels for 0%

profile of v1, /device:TPU:0, one launch (start us, length us, event | category | flops | bytes accessed | tf_op | source)
XLA Modules:
  0.0 209.4 jit_solution(13729498884485307832)
XLA Ops:
  7.2 8.1 %fusion.64 = (f32[32,32,8,1]{3,2,1,0:T(8,128)}, f32[32,32,8,1]{3,2,1,0:T(8,128)}) fusion(f32[32,32,8,128]{3,2,1,0:T(8,128)} %param.11), kind=kLoop, calls=%fused_computation.101 | loop fusion | bytes 131072 | tf_op jit(solution)/shard_map/slice | solution.py:19
  15.3 3.2 %copy.180 = f32[32,32,8,1]{1,2,3,0:T(8,128)S(1)} copy(f32[32,32,8,1]{3,2,1,0:T(8,128)} %get-tuple-element.14) | data formatting | bytes 65536
  18.6 3.0 %collective-permute-start = (f32[32,32,8,1]{1,2,3,0:T(8,128)S(1)}, f32[32,32,8,1]{1,2,3,0:T(8,128)}, u32[]{:S(2)}, u32[]{:S(2)}) collective-permute-start(f32[32,32,8,1]{1,2,3,0:T(8,128)S(1)} %copy.180), channel_id=1, source_target_pairs={{0,4},{4,8},{8,12},{12,16},{16,20},{20,24},{24,28},{28,0},{1,5},{5... | collective-permute-start | bytes 98312 | tf_op jit(solution)/shard_map/ppermute | solution.py:21
  21.6 3.8 %copy.181 = f32[32,32,8,1]{1,2,3,0:T(8,128)} copy(f32[32,32,8,1]{3,2,1,0:T(8,128)} %get-tuple-element.15) | data formatting | bytes 65536
  25.5 3.1 %collective-permute-start.1 = (f32[32,32,8,1]{1,2,3,0:T(8,128)}, f32[32,32,8,1]{1,2,3,0:T(8,128)}, u32[]{:S(2)}, u32[]{:S(2)}) collective-permute-start(f32[32,32,8,1]{1,2,3,0:T(8,128)} %copy.181), channel_id=1, source_target_pairs={{4,0},{8,4},{12,8},{16,12},{20,16},{24,20},{28,24},{0,28},{5,1},{9... | collective-permute-start | bytes 98312 | tf_op jit(solution)/shard_map/ppermute | solution.py:22
  28.6 5.4 %fusion.65 = (f32[32,32,1,128]{3,2,1,0:T(1,128)}, f32[32,32,1,128]{3,2,1,0:T(1,128)}) fusion(f32[32,32,8,128]{3,2,1,0:T(8,128)} %param.11), kind=kLoop, calls=%fused_computation.102 | loop fusion | bytes 2097152 | tf_op jit(solution)/shard_map/slice | solution.py:19
  34.0 1.5 collective-permute-start.2
  35.5 1.3 collective-permute-start.3
  36.8 0.9 broadcast_maximum_fusion
  38.5 3.8 %copy.159 = f32[32,32,8,1]{3,2,1,0:T(8,128)} copy(f32[32,32,8,1]{1,2,3,0:T(8,128)} %collective-permute-done) | data formatting | bytes 65536 | tf_op jit(solution)/shard_map/ppermute | solution.py:21
  42.3 3.8 %copy.161 = f32[32,32,8,1]{3,2,1,0:T(8,128)} copy(f32[32,32,8,1]{1,2,3,0:T(8,128)} %collective-permute-done.1) | data formatting | bytes 65536 | tf_op jit(solution)/shard_map/ppermute | solution.py:22
  46.1 12.7 %fusion.19 = f32[32,32,8,128]{3,2,1,0:T(8,128)S(1)} fusion(f32[32,32,8,128]{3,2,1,0:T(8,128)} %param.11, f32[32,32,1,128]{3,2,1,0:T(1,128)S(1)} %bitcast.69, f32[32,32,1,128]{3,2,1,0:T(1,128)S(1)} %bitcast.68, f32[32,32,8,1]{3,2,1,0:T(8,128)} %copy.161, f32[32,32,8,1]{3,2,1,0:T(8,128)} %copy.159, f32[32,8,128]{2,1,0:T(8,128)S(1)} %copy-done.2, ...), kind=kLoop, calls=%fused_computation.27 | loop fusion | flops 18874368 | bytes 10289152 | tf_op jit(solution)/shard_map/add | solution.py:48
  58.8 2.4 %fusion.63 = (f32[32,32,1,128]{3,2,1,0:T(1,128)}, f32[32,32,1,128]{3,2,1,0:T(1,128)}) fusion(f32[32,32,8,128]{3,2,1,0:T(8,128)S(1)} %fusion.19), kind=kLoop, calls=%fused_computation.100 | loop fusion | bytes 2097152 | tf_op jit(solution)/shard_map/slice | solution.py:19
  61.2 4.7 %collective-permute-start.6 = (f32[32,32,1,128]{3,1,2,0:T(8,128)}, f32[32,32,1,128]{3,1,2,0:T(8,128)S(1)}, u32[]{:S(2)}, u32[]{:S(2)}) collective-permute-start(f32[32,32,1,128]{3,1,2,0:T(8,128)} %bitcast.2), channel_id=1, source_target_pairs={{0,1},{1,2},{2,3},{4,5},{5,6},{6,7},{8,9},{9,10},{10,11},{12,13},{... | collective-permute-start | bytes 1572872 | tf_op jit(solution)/shard_map/ppermute | solution.py:21
  65.9 1.3 collective-permute-start.7
  67.2 4.9 %fusion.62 = (f32[32,32,8,1]{3,2,1,0:T(8,128)}, f32[32,32,8,1]{3,2,1,0:T(8,128)}) fusion(f32[32,32,8,128]{3,2,1,0:T(8,128)S(1)} %fusion.19), kind=kLoop, calls=%fused_computation.99 | loop fusion | bytes 131072 | tf_op jit(solution)/shard_map/slice | solution.py:19
  72.1 3.2 %copy.166 = f32[32,32,8,1]{1,2,3,0:T(8,128)S(1)} copy(f32[32,32,8,1]{3,2,1,0:T(8,128)} %get-tuple-element.10) | data formatting | bytes 65536 | tf_op jit(solution)/shard_map/slice | solution.py:19
  75.3 3.8 %copy.168 = f32[32,32,8,1]{1,2,3,0:T(8,128)} copy(f32[32,32,8,1]{3,2,1,0:T(8,128)} %get-tuple-element.11) | data formatting | bytes 65536 | tf_op jit(solution)/shard_map/slice | solution.py:20
  79.2 4.7 %collective-permute-start.5 = (f32[32,32,8,1]{1,2,3,0:T(8,128)}, f32[32,32,8,1]{1,2,3,0:T(8,128)}, u32[]{:S(2)}, u32[]{:S(2)}) collective-permute-start(f32[32,32,8,1]{1,2,3,0:T(8,128)} %copy.168), channel_id=1, source_target_pairs={{4,0},{8,4},{12,8},{16,12},{20,16},{24,20},{28,24},{0,28},{5,1},{9... | collective-permute-start | bytes 98312 | tf_op jit(solution)/shard_map/ppermute | solution.py:22
  83.9 3.8 %copy.167 = f32[32,32,8,1]{3,2,1,0:T(8,128)} copy(f32[32,32,8,1]{1,2,3,0:T(8,128)} %collective-permute-done.4) | data formatting | bytes 65536 | tf_op jit(solution)/shard_map/ppermute | solution.py:21
  87.7 3.8 %copy.169 = f32[32,32,8,1]{3,2,1,0:T(8,128)} copy(f32[32,32,8,1]{1,2,3,0:T(8,128)} %collective-permute-done.5) | data formatting | bytes 65536 | tf_op jit(solution)/shard_map/ppermute | solution.py:22
  91.5 15.0 %fusion.60 = (f32[32,8,128]{2,1,0:T(8,128)S(1)}, f32[32,8,128]{2,1,0:T(8,128)S(1)}, f32[32,32,8,128]{3,2,1,0:T(8,128)}) fusion(f32[32,8,128]{2,1,0:T(8,128)S(1)} %copy-done.2, f32[32,32,8,128]{3,2,1,0:T(8,128)} %copy-done.1, f32[32,32,1,128]{3,2,1,0:T(1,128)S(1)} %bitcast.67, f32[32,8,128]{2,1,0:T(8,128)S(1)} %get-tuple-element.21, ...), kind=kLoop, calls=%fused_computation.98 | loop fusion | flops 20905984 | bytes 10551296 | tf_op jit(solution)/shard_map/reduce_sum | solution.py:124
  107.8 1.0 fusion.32
  109.6 23.5 %reduce-scatter.2.cloned.1.call-done = f32[32,512]{1,0:T(8,128)} async-done(((f32[32,2048]{1,0:T(8,128)}), f32[32,512]{1,0:T(8,128)}) %reduce-scatter.2.cloned.1.call-update) | async-done | bytes 65552 | tf_op jit(solution)/shard_map/reduce_scatter | solution.py:117
  134.6 1.1 fusion.40
  135.8 1.0 convolution_bitcast_fusion
  136.7 10.3 %all-reduce.1 = (f32[32,32]{1,0:T(8,128)S(1)}, f32[32]{0:T(128)S(1)}) all-reduce(f32[32,32]{1,0:T(8,128)S(1)} %fusion.40, f32[32]{0:T(128)S(1)} %convolution_bitcast_fusion), channel_id=1, replica_groups=mesh['lon'=8,'lat'=4] {'lat'}, use_global_device_ids=true, to_apply=%region_4.5 | all-reduce | flops 1056 | bytes 8448 | tf_op jit(solution)/shard_map/psum | solution.py:121
  147.0 37.2 %all-reduce = (f32[32,32]{1,0:T(8,128)S(1)}, f32[32]{0:T(128)S(1)}) all-reduce(f32[32,32]{1,0:T(8,128)S(1)} %get-tuple-element.7, f32[32]{0:T(128)S(1)} %get-tuple-element.8), channel_id=1, replica_groups=mesh['lon'=8,'lat'=4] {'lon'}, use_global_device_ids=true, to_apply=%region_5.6 | all-reduce | flops 1056 | bytes 8448 | tf_op jit(solution)/shard_map/psum | solution.py:121
  184.3 2.9 %cholesky.17 = f32[32,32]{1,0:T(8,128)S(1)} custom-call(f32[32,32]{1,0:T(8,128)S(1)} %fusion.51), custom_call_target="Cholesky" | custom-call | tf_op jit(solution)/shard_map/jit(cholesky)/cholesky | solution.py:54
  188.5 2.4 %custom-call.10 = f32[1,32,32]{1,2,0:T(8,128)S(1)} custom-call(f32[1,32,32]{2,1,0:T(8,128)S(1)} %fusion.47), custom_call_target="InvertDiagBlocksLowerTriangular" | custom-call | tf_op jit(solution)/shard_map/triangular_solve | solution.py:56
  191.5 8.3 %fusion.29 = f32[4,8,256,128]{3,1,2,0:T(8,128)S(1)} fusion(f32[32,32]{1,0:T(8,128)S(1)} %fusion.31, f32[4,8,256,128]{3,2,1,0:T(8,128)} %bitcast.62, f32[32768]{0:T(1024)S(1)} %multiply_bitcast_fusion), kind=kOutput, calls=%fused_computation.40 | convolution fusion | flops 404750336 | bytes 8523776 | tf_op jit(solution)/shard_map/dot_general | solution.py:126
  199.8 2.8 %copy.186 = f32[4,8,256,128]{3,2,1,0:T(8,128)} copy(f32[4,8,256,128]{3,1,2,0:T(8,128)S(1)} %fusion.29) | data formatting | bytes 8388608
  (50 shorter events, 5.6 us)
Async XLA Ops:
  7.2 100.1 %copy-start = (bf16[48,128,128]{2,1,0:T(8,128)(2,1)S(1)}, bf16[48,128,128]{2,1,0:T(8,128)(2,1)}, u32[]{:S(2)}) copy-start(bf16[48,128,128]{2,1,0:T(8,128)(2,1)} %param.19) | copy-start | bytes 4718596
  7.2 126.0 %reduce-scatter.2.cloned.1.call-start = ((), (), s32[]{:S(2)}) async-start(), calls=%async_computation.1 | async-start | bytes 327680 | tf_op jit(solution)/shard_map/reduce_scatter | solution.py:117
  18.6 18.2 %copy-start.3 = (f32[32,8,128]{2,1,0:T(8,128)S(1)}, f32[32,8,128]{2,1,0:T(8,128)}, u32[]{:S(2)}) copy-start(f32[32,8,128]{2,1,0:T(8,128)} %param.15) | copy-start | bytes 393220
  18.6 18.2 %copy-start.8 = (s32[48]{0:T(128)S(1)}, s32[48]{0:T(128)}, u32[]{:S(2)}) copy-start(s32[48]{0:T(128)} %param.17) | copy-start | bytes 580
  18.6 18.3 %copy-start.4 = (f32[32,8,128]{2,1,0:T(8,128)S(1)}, f32[32,8,128]{2,1,0:T(8,128)}, u32[]{:S(2)}) copy-start(f32[32,8,128]{2,1,0:T(8,128)} %param.13) | copy-start | bytes 393220
  18.6 19.9 %collective-permute-start = (f32[32,32,8,1]{1,2,3,0:T(8,128)S(1)}, f32[32,32,8,1]{1,2,3,0:T(8,128)}, u32[]{:S(2)}, u32[]{:S(2)}) collective-permute-start(f32[32,32,8,1]{1,2,3,0:T(8,128)S(1)} %copy.180), channel_id=1, source_target_pairs={{0,4},{4,8},{8,12},{12,16},{16,20},{20,24},{24,28},{28,0},{1,5},{5... | collective-permute-start | bytes 98312 | tf_op jit(solution)/shard_map/ppermute | solution.py:21
  25.5 16.8 %collective-permute-start.1 = (f32[32,32,8,1]{1,2,3,0:T(8,128)}, f32[32,32,8,1]{1,2,3,0:T(8,128)}, u32[]{:S(2)}, u32[]{:S(2)}) collective-permute-start(f32[32,32,8,1]{1,2,3,0:T(8,128)} %copy.181), channel_id=1, source_target_pairs={{4,0},{8,4},{12,8},{16,12},{20,16},{24,20},{28,24},{0,28},{5,1},{9... | collective-permute-start | bytes 98312 | tf_op jit(solution)/shard_map/ppermute | solution.py:22
  34.0 12.1 %collective-permute-start.2 = (f32[32,32,1,128]{3,1,2,0:T(8,128)}, f32[32,32,1,128]{3,1,2,0:T(8,128)S(1)}, u32[]{:S(2)}, u32[]{:S(2)}) collective-permute-start(f32[32,32,1,128]{3,1,2,0:T(8,128)} %bitcast.20), channel_id=1, source_target_pairs={{0,1},{1,2},{2,3},{4,5},{5,6},{6,7},{8,9},{9,10},{10,11},{12,13},{... | collective-permute-start | bytes 1572872 | tf_op jit(solution)/shard_map/ppermute | solution.py:21
  35.5 10.7 %collective-permute-start.3 = (f32[32,32,1,128]{3,1,2,0:T(8,128)}, f32[32,32,1,128]{3,1,2,0:T(8,128)S(1)}, u32[]{:S(2)}, u32[]{:S(2)}) collective-permute-start(f32[32,32,1,128]{3,1,2,0:T(8,128)} %bitcast.21), channel_id=1, source_target_pairs={{1,0},{2,1},{3,2},{5,4},{6,5},{7,6},{9,8},{10,9},{11,10},{13,12},{... | collective-permute-start | bytes 1572872 | tf_op jit(solution)/shard_map/ppermute | solution.py:22
  38.5 7.7 %copy-start.2 = (f32[32,8,128]{2,1,0:T(8,128)S(1)}, f32[32,8,128]{2,1,0:T(8,128)}, u32[]{:S(2)}) copy-start(f32[32,8,128]{2,1,0:T(8,128)} %param.14) | copy-start | bytes 393220
  58.8 13.2 %copy-start.1 = (f32[32,32,8,128]{3,2,1,0:T(8,128)}, f32[32,32,8,128]{3,2,1,0:T(8,128)S(1)}, u32[]{:S(2)}) copy-start(f32[32,32,8,128]{3,2,1,0:T(8,128)S(1)} %fusion.19) | copy-start | bytes 12582916
  61.2 30.4 %collective-permute-start.6 = (f32[32,32,1,128]{3,1,2,0:T(8,128)}, f32[32,32,1,128]{3,1,2,0:T(8,128)S(1)}, u32[]{:S(2)}, u32[]{:S(2)}) collective-permute-start(f32[32,32,1,128]{3,1,2,0:T(8,128)} %bitcast.2), channel_id=1, source_target_pairs={{0,1},{1,2},{2,3},{4,5},{5,6},{6,7},{8,9},{9,10},{10,11},{12,13},{... | collective-permute-start | bytes 1572872 | tf_op jit(solution)/shard_map/ppermute | solution.py:21
  65.9 25.7 %collective-permute-start.7 = (f32[32,32,1,128]{3,1,2,0:T(8,128)}, f32[32,32,1,128]{3,1,2,0:T(8,128)S(1)}, u32[]{:S(2)}, u32[]{:S(2)}) collective-permute-start(f32[32,32,1,128]{3,1,2,0:T(8,128)} %bitcast.4), channel_id=1, source_target_pairs={{1,0},{2,1},{3,2},{5,4},{6,5},{7,6},{9,8},{10,9},{11,10},{13,12},{... | collective-permute-start | bytes 1572872 | tf_op jit(solution)/shard_map/ppermute | solution.py:22
  75.3 8.6 %collective-permute-start.4 = (f32[32,32,8,1]{1,2,3,0:T(8,128)S(1)}, f32[32,32,8,1]{1,2,3,0:T(8,128)}, u32[]{:S(2)}, u32[]{:S(2)}) collective-permute-start(f32[32,32,8,1]{1,2,3,0:T(8,128)S(1)} %copy.166), channel_id=1, source_target_pairs={{0,4},{4,8},{8,12},{12,16},{16,20},{20,24},{24,28},{28,0},{1,5},{5... | collective-permute-start | bytes 98312 | tf_op jit(solution)/shard_map/ppermute | solution.py:21
  79.2 8.5 %collective-permute-start.5 = (f32[32,32,8,1]{1,2,3,0:T(8,128)}, f32[32,32,8,1]{1,2,3,0:T(8,128)}, u32[]{:S(2)}, u32[]{:S(2)}) collective-permute-start(f32[32,32,8,1]{1,2,3,0:T(8,128)} %copy.168), channel_id=1, source_target_pairs={{4,0},{8,4},{12,8},{16,12},{20,16},{24,20},{28,24},{0,28},{5,1},{9... | collective-permute-start | bytes 98312 | tf_op jit(solution)/shard_map/ppermute | solution.py:22
  91.5 16.3 %copy-start.7 = (s32[48]{0:T(128)S(1)}, s32[48]{0:T(128)}, u32[]{:S(2)}) copy-start(s32[48]{0:T(128)} %param.18) | copy-start | bytes 580
  106.5 27.5 %copy-start.5 = (f32[512]{0:T(512)S(1)}, f32[512]{0:T(512)}, u32[]{:S(2)}) copy-start(f32[512]{0:T(512)} %param.20) | copy-start | bytes 6148
  106.5 27.5 %copy-start.6 = (f32[512]{0:T(512)S(1)}, f32[512]{0:T(512)}, u32[]{:S(2)}) copy-start(f32[512]{0:T(512)} %param.21) | copy-start | bytes 6148
Sparse Core Ops, SparseCore 0:
  109.7 23.3 reduce-scatter.1
